TPU v7x, 256 devices: a whole 4x4x8 slice. The times are simulated.
256 devices in a mesh: rows: 32 (over x, z_lo, core), cols: 8 (over y, z_hi).
Axes of the slice: x: 4, y: 4, z: 8 (z_hi: 2, z_lo: 4; z = z_hi * 4 + z_lo), core: 2. Of those that a mesh axis runs over, the one named last changes fastest.
Arguments:
- matrix_blocks: bfloat16 [8192, 64, 1728], P(('rows', 'cols')), may hold values from -0.75 to 0.75
- restrict: bfloat16 [8192, 4096], P(('rows', 'cols')), may hold values from -1.5 to 1.5
- columns: int32 [8192, 27], P(('rows', 'cols')), may hold values from 0 to 767
- counts: int32 [8192], P(('rows', 'cols')), may hold values from 8 to 27, as said below
- aggregate: int32 [8192], P(('rows', 'cols')), may hold values from 0 to 1
Outputs:
- coarse: float32 [512, 64, 3072], P(('rows', 'cols'))
Inputs may be any that keep to these rules, and one draw needn't show every extreme that they name: `counts`: used slots are the first ones of a row; some row uses all 27.
All inputs are finite; a program needn't handle non-finite values.
Results may differ from a plain program's by a relative error of at most 0.0029.
Values may be sent and summed in bfloat16 or wider, within the bound.
A program may use at most 192 MiB of HBM per device.

v0:
```python
import jax
import jax.numpy as jnp
from jax import lax
from jax.sharding import PartitionSpec as P

BLK = 64
SLOTS = 27
ROWS_DEV = 32
AGG_DEV = 2


def padded(block, sides, width):
    for axis, dim in sides:
        count = lax.axis_size(axis)
        forward = [(i, i + 1) for i in range(count - 1)]
        backward = [(target, source) for source, target in forward]
        low = lax.ppermute(
            lax.slice_in_dim(block, block.shape[dim] - width, None, axis=dim), axis, forward
        )
        high = lax.ppermute(lax.slice_in_dim(block, 0, width, axis=dim), axis, backward)
        block = jnp.concatenate([low, block, high], axis=dim)
    return block


def per_device(matrix_blocks, restrict, columns, counts, aggregate):
    col_count = lax.axis_size("cols")
    row_count = lax.axis_size("rows")
    slab_index = lax.axis_index("rows")
    slab_rows = ROWS_DEV * col_count
    window = 3 * AGG_DEV * col_count
    slab_blocks, slab_aggs = (
        lax.all_gather(restrict, "cols", axis=0, tiled=True),
        lax.all_gather(aggregate, "cols", axis=0, tiled=True),
    )
    near_blocks, near_aggs = (
        padded(slab_blocks, (("rows", 0),), slab_rows),
        padded(slab_aggs, (("rows", 0),), slab_rows),
    )
    slot_index = jnp.arange(SLOTS, dtype=jnp.int32)
    inside = ((columns >= slab_rows) | (slab_index > 0)) & (
        (columns < 2 * slab_rows) | (slab_index < row_count - 1)
    )
    live_mask = ((slot_index[None, :] < counts[:, None]) & inside).astype(jnp.float32)
    slot_ids = columns // ROWS_DEV * AGG_DEV + near_aggs[columns]
    segment = aggregate[:, None] * window + slot_ids
    targets = jnp.arange(AGG_DEV * window, dtype=jnp.int32)
    one_hot = (segment[:, :, None] == targets[None, None, :]).astype(jnp.float32) * live_mask[
        :, :, None
    ]
    own_blocks = restrict.reshape(ROWS_DEV, BLK, BLK)
    left_prod = jnp.einsum(
        "ips,isn->ipn", own_blocks, matrix_blocks, preferred_element_type=jnp.float32
    )
    left_prod = left_prod.astype(jnp.bfloat16).reshape(ROWS_DEV, BLK, SLOTS, BLK)
    far_blocks = near_blocks[columns.reshape(-1)].reshape(ROWS_DEV, SLOTS, BLK, BLK)
    products = jnp.einsum(
        "ipks,ikqs->ikpq", left_prod, far_blocks, preferred_element_type=jnp.float32
    )
    summed = jnp.einsum(
        "ikm,ikpq->mpq",
        one_hot,
        products,
        precision=lax.Precision.HIGHEST,
        preferred_element_type=jnp.float32,
    )
    return (
        summed.reshape(AGG_DEV, window, BLK, BLK)
        .transpose(0, 2, 1, 3)
        .reshape(AGG_DEV, BLK, window * BLK)
    )


def solution(mesh):
    return jax.shard_map(
        per_device,
        mesh=mesh,
        in_specs=(
            P(("rows", "cols"), None, None),
            P(("rows", "cols"), None),
            P(("rows", "cols"), None),
            P(("rows", "cols")),
            P(("rows", "cols")),
        ),
        out_specs=P(("rows", "cols"), None, None),
        check_vma=False,
    )
```

profile of v0, /device:TPU:31, one launch (start us, length us, event | category | flops | bytes accessed | tf_op | source)
XLA Modules:
  0.0 335.7 jit_solution(14347546717908960223)
XLA Ops:
  6.5 0.7 all-gather.2.cloned.1.call-update
  7.3 73.9 %all-gather.2.cloned.1.call-done = bf16[256,4096]{1,0:T(8,128)(2,1)} async-done(((bf16[32,4096]{1,0:T(8,128)(2,1)}), bf16[256,4096]{1,0:T(8,128)(2,1)}) %all-gather.2.cloned.1.call-update) | async-done | bytes 2097168 | tf_op jit(solution)/shard_map/all_gather | solution.py:32
  81.1 9.7 %collective-permute-start.3 = (bf16[256,4096]{1,0:T(8,128)(2,1)}, bf16[256,4096]{1,0:T(8,128)(2,1)}, u32[]{:S(2)}, u32[]{:S(2)}) collective-permute-start(bf16[256,4096]{1,0:T(8,128)(2,1)} %all-gather.2.cloned.1.call-done), channel_id=1, source_target_pairs={{8,0},{16,8},{24,16},{32,24},{40,32},{48,40},{56,48},{64,56},{72,6... | collective-permute-start | bytes 6291464 | tf_op jit(solution)/shard_map/ppermute | solution.py:20
  90.8 2.2 collective-permute-start.2
  93.1 1.3 dynamic-slice
  95.0 0.9 dynamic-update-slice
  95.8 45.3 %all-reduce = s32[256]{0:T(256)S(1)} all-reduce(s32[256]{0:T(256)S(1)} %dynamic-update-slice), channel_id=1, replica_groups=mesh['rows'=32,'cols'=8] {'cols'}, use_global_device_ids=true, to_apply=%add | all-reduce | flops 256 | bytes 2048
  141.1 1.9 collective-permute-start.1
  143.1 3.6 %collective-permute-start = (s32[256]{0:T(256)S(1)}, s32[256]{0:T(256)S(1)}, u32[]{:S(2)}, u32[]{:S(2)}) collective-permute-start(s32[256]{0:T(256)S(1)} %all-reduce), channel_id=1, source_target_pairs={{0,8},{8,16},{16,24},{24,32},{32,40},{40,48},{48,56},{56,64},{64,7... | collective-permute-start | bytes 3080 | tf_op jit(solution)/shard_map/ppermute | solution.py:17
  146.7 1.5 reshape.51
  148.2 0.8 reshape.53
  149.0 0.7 add_select_fusion
  149.7 0.1 reshape.59
  149.9 0.7 broadcast_multiply_fusion
  150.5 0.8 fusion.18
  151.3 8.1 %convolution_convert_fusion = bf16[32,64,1728]{2,1,0:T(8,128)(2,1)} fusion(bf16[32,64,64]{2,1,0:T(8,128)(2,1)S(1)} %reshape.51, bf16[32,64,1728]{2,1,0:T(8,128)(2,1)} %param.5), kind=kOutput, calls=%fused_computation.7 | convolution fusion | flops 456523776 | bytes 14417920 | tf_op jit(solution)/shard_map/ips,isn->ipn/dot_general | solution.py:51
  159.4 22.9 %reshape.52 = bf16[32,64,27,64]{3,2,1,0:T(8,128)(2,1)} reshape(bf16[32,64,1728]{2,1,0:T(8,128)(2,1)} %convolution_convert_fusion) | data formatting | bytes 14155776 | tf_op jit(solution)/shard_map/reshape | solution.py:54
  182.4 0.1 copy.13
  182.4 0.0 collective-permute-done.1
  182.5 0.0 copy-start.1
  182.5 3.7 %gather_fusion = s32[864]{0:T(1024)S(1)} fusion(s32[768]{0:T(1024)S(1)} %pad_add_fusion, s32[1024]{0:T(1024)S(1)} %pad_clamp_fusion.1), kind=kCustom, calls=%fused_computation | custom fusion | bytes 10368 | tf_op jit(solution)/shard_map/gather | solution.py:44
  186.2 0.1 reshape.58
  186.3 0.1 fusion.15
  186.3 0.1 copy.12
  186.4 5.5 %pad_maximum_fusion = bf16[768,4096]{1,0:T(8,128)(2,1)} fusion(bf16[256,4096]{1,0:T(8,128)(2,1)} %collective-permute-done.3, bf16[256,4096]{1,0:T(8,128)(2,1)S(1)} %copy-done, bf16[256,4096]{1,0:T(8,128)(2,1)} %collective-permute-done.2), kind=kLoop, calls=%fused_computation.6 | loop fusion | flops 18874368 | bytes 12582912 | tf_op jit(solution)/shard_map/concatenate | solution.py:21
  191.9 18.5 %gather_fusion.1 = bf16[864,4096]{1,0:T(8,128)(2,1)} fusion(bf16[768,4096]{1,0:T(8,128)(2,1)} %pad_maximum_fusion, s32[1024]{0:T(1024)S(1)} %pad_clamp_fusion), kind=kCustom, calls=%fused_computation.1 | custom fusion | bytes 14159232 | tf_op jit(solution)/shard_map/gather | solution.py:55
  210.4 20.0 %reshape.54 = bf16[32,27,64,64]{3,2,1,0:T(8,128)(2,1)} reshape(bf16[864,4096]{1,0:T(8,128)(2,1)} %gather_fusion.1) | data formatting | bytes 14155776 | tf_op jit(solution)/shard_map/reshape | solution.py:55
  230.3 23.6 %fusion.2 = f32[32,27,64,64]{3,2,1,0:T(8,128)} fusion(bf16[32,27,64,64]{3,2,1,0:T(8,128)(2,1)} %reshape.54, bf16[32,64,27,64]{3,2,1,0:T(8,128)(2,1)} %reshape.52), kind=kOutput, calls=%fused_computation.4 | convolution fusion | flops 452984832 | bytes 28311552 | tf_op jit(solution)/shard_map/ipks,ikqs->ikpq/dot_general | solution.py:56
  254.0 64.2 %fusion.4 = f32[96,64,64]{0,2,1:T(8,128)} fusion(f32[32,27,64,64]{3,2,1,0:T(8,128)} %fusion.2, f32[32,27]{0,1:T(8,128)S(1)} %copy.13, s32[32,27]{0,1:T(8,128)S(1)} %copy.12), kind=kOutput, calls=%fused_computation.8 | convolution fusion | flops 4077029376 | bytes 15735552 | tf_op jit(solution)/shard_map/ikm,ikpq->mpq/dot_general | solution.py:59
  318.1 4.0 %copy.16 = f32[96,64,64]{2,1,0:T(8,128)S(1)} copy(f32[96,64,64]{0,2,1:T(8,128)} %fusion.4) | data formatting | bytes 3145728 | tf_op jit(solution)/shard_map/ikm,ikpq->mpq/dot_general | solution.py:59
  322.2 3.5 %copy.17 = f32[2,64,48,64]{3,2,1,0:T(8,128)} copy(f32[2,64,48,64]{3,1,2,0:T(8,128)S(1)} %bitcast.15) | data formatting | bytes 3145728 | tf_op jit(solution)/shard_map/transpose | solution.py:68
  325.6 3.2 reshape.56
  (12 shorter events, 0.1 us)
Async XLA Ops:
  6.5 74.6 %all-gather.2.cloned.1.call-start = ((), (), s32[]{:S(2)}) async-start(), calls=%async_computation | async-start | bytes 2359296 | tf_op jit(solution)/shard_map/all_gather | solution.py:32
  81.1 105.3 %collective-permute-start.3 = (bf16[256,4096]{1,0:T(8,128)(2,1)}, bf16[256,4096]{1,0:T(8,128)(2,1)}, u32[]{:S(2)}, u32[]{:S(2)}) collective-permute-start(bf16[256,4096]{1,0:T(8,128)(2,1)} %all-gather.2.cloned.1.call-done), channel_id=1, source_target_pairs={{8,0},{16,8},{24,16},{32,24},{40,32},{48,40},{56,48},{64,56},{72,6... | collective-permute-start | bytes 6291464 | tf_op jit(solution)/shard_map/ppermute | solution.py:20
  90.8 95.6 %collective-permute-start.2 = (bf16[256,4096]{1,0:T(8,128)(2,1)}, bf16[256,4096]{1,0:T(8,128)(2,1)}, u32[]{:S(2)}, u32[]{:S(2)}) collective-permute-start(bf16[256,4096]{1,0:T(8,128)(2,1)} %all-gather.2.cloned.1.call-done), channel_id=1, source_target_pairs={{0,8},{8,16},{16,24},{24,32},{32,40},{40,48},{48,56},{56,64},{64,7... | collective-permute-start | bytes 6291464 | tf_op jit(solution)/shard_map/ppermute | solution.py:17
  141.1 41.3 %collective-permute-start.1 = (s32[256]{0:T(256)S(1)}, s32[256]{0:T(256)S(1)}, u32[]{:S(2)}, u32[]{:S(2)}) collective-permute-start(s32[256]{0:T(256)S(1)} %all-reduce), channel_id=1, source_target_pairs={{8,0},{16,8},{24,16},{32,24},{40,32},{48,40},{56,48},{64,56},{72,6... | collective-permute-start | bytes 3080 | tf_op jit(solution)/shard_map/ppermute | solution.py:20
  143.1 39.4 %collective-permute-start = (s32[256]{0:T(256)S(1)}, s32[256]{0:T(256)S(1)}, u32[]{:S(2)}, u32[]{:S(2)}) collective-permute-start(s32[256]{0:T(256)S(1)} %all-reduce), channel_id=1, source_target_pairs={{0,8},{8,16},{16,24},{24,32},{32,40},{40,48},{48,56},{56,64},{64,7... | collective-permute-start | bytes 3080 | tf_op jit(solution)/shard_map/ppermute | solution.py:17
  182.5 3.8 %copy-start.1 = (s32[32,27]{1,0:T(8,128)S(1)}, s32[32,27]{1,0:T(8,128)}, u32[]{:S(2)}) copy-start(s32[32,27]{1,0:T(8,128)} %param.7) | copy-start | bytes 10372
  182.5 4.0 %copy-start = (bf16[256,4096]{1,0:T(8,128)(2,1)S(1)}, bf16[256,4096]{1,0:T(8,128)(2,1)}, u32[]{:S(2)}) copy-start(bf16[256,4096]{1,0:T(8,128)(2,1)} %all-gather.2.cloned.1.call-done) | copy-start | bytes 6291460
Sparse Core Ops, SparseCore 0:
  10.0 71.1 all-gather.1
where the time goes:
time: 339 us; the launch traced here: 336 us
  matrix products  95.9 us (28%)
  local copies, waits for them, and re-layouts  80.5 us (24%)
  waiting for transfers between devices  74.6 us (22%)
  blocking collectives  45.3 us (13%)
  starting transfers between devices  17.5 us (5%)
  between operations  14.2 us (4%)
  other arithmetic  7.74 us (2%)
    all_gather x1, waiting for transfers between devices, per_device(): lax.all_gather(restrict, 'cols', axis=0, tiled=True)  73.9 us
    dot_general x1, matrix products, per_device(): jnp.einsum('ikm,ikpq->mpq', one_hot, products, precision=lax.Precision.HI...  64.2 us
    unnamed x1, blocking collectives  45.3 us
    dot_general x1, matrix products, per_device(): jnp.einsum('ipks,ikqs->ikpq', left_prod, far_blocks, preferred_element_ty...  23.6 us
    reshape x1, local copies, waits for them, and re-layouts, per_device(): left_prod.astype(jnp.bfloat16).reshape(ROWS_DEV, BLK, SLOTS, BLK)  22.9 us
    reshape x1, local copies, waits for them, and re-layouts, per_device(): near_blocks[columns.reshape(-1)].reshape(ROWS_DEV, SLOTS, BLK, BLK)  20 us
    gather x1, local copies, waits for them, and re-layouts, per_device(): near_blocks[columns.reshape(-1)].reshape(ROWS_DEV, SLOTS, BLK, BLK)  18.5 us
    ppermute x2, starting transfers between devices, padded(): lax.ppermute(lax.slice_in_dim(block, 0, width, axis=dim), axis, backward)  11.6 us
  transfers between devices with their start and end apart: 5, of which 1 were waited for; matrix products, arithmetic and copies ran while one was open for 12% of the time, Pallas kernels for 0%

commit v1 on v0

v1 whole, which is shorter than its diff:
```python
import functools

import jax
import jax.numpy as jnp
from jax import lax
from jax.experimental import pallas as pl
from jax.experimental.pallas import tpu as pltpu
from jax.sharding import PartitionSpec as P

BLK = 64
SLOTS = 27
ROWS_DEV = 32
AGG_DEV = 2
Y = 4
NZ = 4
TILES = ROWS_DEV // 2
LTILES = (SLOTS + 1) // 2
PIECE = TILES * 4 + 1
MESH = pl.DeviceIdType.MESH


def gather_kernel(n_rows, with_left, x_ref, a_hbm, g_ref, l_hbm, a_buf, l_buf, send_sem, recv_sem, own_sem, a_sem, l_sem):
    r = lax.axis_index("rows")
    col = lax.axis_index("cols")
    y = col // 2
    zh = lax.rem(col, 2)
    c = lax.rem(r, 2)
    zlo = lax.rem(r // 2, NZ)
    d = 1 - 2 * c
    partner = r + d
    far = r - d
    has_far = jnp.logical_and(far >= 0, far < n_rows)
    turn = jnp.logical_or(
        jnp.logical_and(zlo == 0, c == 0), jnp.logical_and(zlo == NZ - 1, c == 1)
    ).astype(jnp.int32)
    near_z = lax.rem(zh + turn, 2)
    other_z = 1 - near_z
    t3 = jnp.where(has_far, far, r)
    z3 = jnp.where(has_far, other_z, 1 - zh)
    r3_row = jnp.where(has_far, far, partner)
    r3_z = jnp.where(has_far, near_z, zh)

    def ring(step):
        return lax.rem(y + step + 2 * Y, Y)

    yf, yb, y2 = ring(d), ring(-d), ring(2)

    def dev(row, yy, zz):
        return (row, yy * 2 + zz)

    me_near = dev(far, y, near_z)
    me_other = dev(t3, y, z3)
    me_part = dev(partner, y, zh)
    me_yf = dev(r, yf, zh)
    me_yb = dev(r, yb, zh)
    me_r3 = dev(r3_row, y, r3_z)

    def slot(row, slab, yy, zz):
        return (slab - row + 1) * (2 * Y) + yy * 2 + zz

    def copy(src, slab, yy, zz, to, index):
        return pltpu.make_async_remote_copy(
            src_ref=src,
            dst_ref=g_ref.at[slot(to[0], slab, yy, zz)],
            send_sem=send_sem.at[index],
            recv_sem=recv_sem.at[slot(to[0], slab, yy, zz)],
            device_id=to,
            device_id_type=MESH,
        )

    def own_copy(to, index):
        return copy(x_ref, r, y, zh, to, index)

    def relay(slab, yy, zz, to, index):
        return copy(g_ref.at[slot(r, slab, yy, zz)], slab, yy, zz, to, index)

    def arrived(slab, yy, zz):
        s = slot(r, slab, yy, zz)
        pltpu.make_async_remote_copy(
            src_ref=g_ref.at[s],
            dst_ref=g_ref.at[s],
            send_sem=send_sem.at[0],
            recv_sem=recv_sem.at[s],
            device_id=me_part,
            device_id_type=MESH,
        ).wait_recv()

    groups = ROWS_DEV // 4

    def a_copy(k):
        rows = pl.ds(k * 4, 4)
        return pltpu.make_async_copy(a_hbm.at[rows], a_buf.at[rows], a_sem.at[k])

    def l_copy(k):
        rows = pl.ds(k * 4, 4)
        return pltpu.make_async_copy(l_buf.at[rows], l_hbm.at[rows], l_sem.at[k])

    if with_left:

        @pl.loop(0, groups)
        def _(k):
            a_copy(k).start()

    barrier = pltpu.get_barrier_semaphore()
    for to in (me_other, me_part, me_yf, me_yb):
        pl.semaphore_signal(barrier, inc=1, device_id=to, device_id_type=MESH)

    @pl.when(has_far)
    def _():
        pl.semaphore_signal(barrier, inc=1, device_id=me_near, device_id_type=MESH)

    pl.semaphore_wait(barrier, 4 + has_far.astype(jnp.int32))

    @pl.when(has_far)
    def _():
        own_copy(me_near, 1).start()

    own_copy(me_other, 0).start()
    own_copy(me_yf, 2).start()
    own_copy(me_yb, 3).start()
    own_copy(me_part, 4).start()
    mine = pltpu.make_async_copy(x_ref, g_ref.at[slot(r, r, y, zh)], own_sem)
    mine.start()

    if with_left:
        low = lax.broadcasted_iota(jnp.int32, (BLK, 128), 1) < BLK
        zero = jnp.zeros((BLK, 128), jnp.bfloat16)

        @pl.loop(0, groups)
        def _(k):
            a_copy(k).wait()
            t0 = x_ref[pl.ds(k * 8, 4)].reshape(BLK, 128)
            t1 = x_ref[pl.ds(k * 8 + 4, 4)].reshape(BLK, 128)
            left_half = jnp.concatenate(
                [jnp.where(low, t0, zero), jnp.where(low, zero, t0), zero, zero], axis=0
            )
            right_half = jnp.concatenate(
                [zero, zero, jnp.where(low, t1, zero), jnp.where(low, zero, t1)], axis=0
            )
            lhs = jnp.concatenate([left_half, right_half], axis=1)
            rows = pl.ds(k * 4, 4)
            for n in range((SLOTS * BLK + 255) // 256):
                width = min(256, SLOTS * BLK - n * 256)
                rhs = a_buf[rows, :, n * 256 : n * 256 + width].reshape(4 * BLK, width)
                prod = jnp.dot(lhs, rhs, preferred_element_type=jnp.float32).astype(jnp.bfloat16)
                l_buf[rows, 2 * n] = prod[:, :128].reshape(4, BLK, 128)
                l_buf[rows, 2 * n + 1, :, : width - 128] = prod[:, 128:].reshape(4, BLK, width - 128)
            l_copy(k).start()

    arrived(r, yb, zh)
    relay(r, yb, zh, me_yf, 10).start()
    relay(r, yb, zh, me_part, 11).start()
    arrived(r, yf, zh)
    relay(r, yf, zh, me_part, 12).start()

    @pl.when(has_far)
    def _():
        arrived(far, y, near_z)
        relay(far, y, near_z, me_yf, 8).start()
        relay(far, y, near_z, me_yb, 9).start()

    arrived(t3, y, z3)
    relay(t3, y, z3, me_yf, 5).start()
    relay(t3, y, z3, me_yb, 6).start()
    relay(t3, y, z3, me_r3, 7).start()
    arrived(r, y2, zh)
    relay(r, y2, zh, me_part, 17).start()
    arrived(t3, yf, z3)
    relay(t3, yf, z3, me_yb, 13).start()
    relay(t3, yf, z3, me_r3, 15).start()
    arrived(t3, yb, z3)
    relay(t3, yb, z3, me_r3, 14).start()

    @pl.when(has_far)
    def _():
        arrived(r, y, 1 - zh)
        relay(r, y, 1 - zh, me_part, 19).start()
        arrived(far, yb, near_z)
        relay(far, yb, near_z, me_yf, 16).start()

    arrived(t3, y2, z3)
    relay(t3, y2, z3, me_r3, 18).start()

    @pl.when(has_far)
    def _():
        arrived(r, yf, 1 - zh)
        relay(r, yf, 1 - zh, me_part, 20).start()
        arrived(r, yb, 1 - zh)
        relay(r, yb, 1 - zh, me_part, 21).start()
        arrived(r, y2, 1 - zh)
        relay(r, y2, 1 - zh, me_part, 22).start()
        arrived(far, yf, near_z)
        arrived(far, y2, near_z)

    for yy in range(Y):
        for zz in range(2):
            arrived(partner, yy, zz)
    mine.wait()

    own_copy(me_other, 0).wait_send()
    own_copy(me_yf, 2).wait_send()
    own_copy(me_yb, 3).wait_send()
    own_copy(me_part, 4).wait_send()
    relay(t3, y, z3, me_yf, 5).wait_send()
    relay(t3, y, z3, me_yb, 6).wait_send()
    relay(t3, y, z3, me_r3, 7).wait_send()
    relay(r, yb, zh, me_yf, 10).wait_send()
    relay(r, yb, zh, me_part, 11).wait_send()
    relay(r, yf, zh, me_part, 12).wait_send()
    relay(t3, yf, z3, me_yb, 13).wait_send()
    relay(t3, yb, z3, me_r3, 14).wait_send()
    relay(t3, yf, z3, me_r3, 15).wait_send()
    relay(r, y2, zh, me_part, 17).wait_send()
    relay(t3, y2, z3, me_r3, 18).wait_send()

    @pl.when(has_far)
    def _():
        own_copy(me_near, 1).wait_send()
        relay(far, y, near_z, me_yf, 8).wait_send()
        relay(far, y, near_z, me_yb, 9).wait_send()
        relay(far, yb, near_z, me_yf, 16).wait_send()
        relay(r, y, 1 - zh, me_part, 19).wait_send()
        relay(r, yf, 1 - zh, me_part, 20).wait_send()
        relay(r, yb, 1 - zh, me_part, 21).wait_send()
        relay(r, y2, 1 - zh, me_part, 22).wait_send()

    if with_left:

        @pl.loop(0, groups)
        def _(k):
            l_copy(k).wait()


def gather(piece, matrix_blocks, n_rows, with_left=True):
    return pl.pallas_call(
        functools.partial(gather_kernel, n_rows, with_left),
        out_shape=(
            jax.ShapeDtypeStruct((6 * Y,) + piece.shape, piece.dtype),
            jax.ShapeDtypeStruct((ROWS_DEV, LTILES, BLK, 128), jnp.bfloat16),
        ),
        in_specs=[pl.BlockSpec(memory_space=pltpu.VMEM), pl.BlockSpec(memory_space=pl.ANY)],
        out_specs=(pl.BlockSpec(memory_space=pl.ANY), pl.BlockSpec(memory_space=pl.ANY)),
        scratch_shapes=[
            pltpu.VMEM((ROWS_DEV, BLK, SLOTS * BLK), jnp.bfloat16),
            pltpu.VMEM((ROWS_DEV, LTILES, BLK, 128), jnp.bfloat16),
            pltpu.SemaphoreType.DMA((23,)),
            pltpu.SemaphoreType.DMA((6 * Y,)),
            pltpu.SemaphoreType.DMA,
            pltpu.SemaphoreType.DMA((ROWS_DEV // 4,)),
            pltpu.SemaphoreType.DMA((ROWS_DEV // 4,)),
        ],
        compiler_params=pltpu.CompilerParams(
            collective_id=0, has_side_effects=True, vmem_limit_bytes=40 << 20
        ),
        name="gather_left",
    )(piece, matrix_blocks)


def entry_kernel(seg_ref, col_ref, count_ref, g_hbm, l_hbm, out_ref, g_buf, l_buf, acc, g_sem, l_sem):
    window = 6 * Y * AGG_DEV
    lane = lax.broadcasted_iota(jnp.int32, (BLK, 128), 1)
    zero = jnp.zeros((BLK, 128), jnp.bfloat16)

    def g_copy(k):
        return pltpu.make_async_copy(g_hbm.at[k], g_buf.at[k], g_sem.at[k])

    def l_copy(k):
        rows = pl.ds(k * 4, 4)
        return pltpu.make_async_copy(l_hbm.at[rows], l_buf.at[rows], l_sem.at[k])

    @pl.loop(0, 6 * Y)
    def _(k):
        g_copy(k).start()

    @pl.loop(0, ROWS_DEV // 4)
    def _(k):
        l_copy(k).start()

    @pl.loop(0, AGG_DEV * window)
    def _(k):
        acc[k] = jnp.zeros((BLK, BLK), jnp.float32)

    @pl.loop(0, 6 * Y)
    def _(k):
        g_copy(k).wait()

    @pl.loop(0, ROWS_DEV // 4)
    def _(k):
        l_copy(k).wait()

    @pl.loop(0, ROWS_DEV)
    def _(i):
        count = count_ref[i]
        for base in range(0, SLOTS, 4):

            @pl.when(base < count)
            def _():
                prods = []
                for k in range(base, min(base + 4, SLOTS)):
                    col = col_ref[i * SLOTS + k]
                    half = lax.rem(col, 2)
                    dev = col // ROWS_DEV
                    tile = lax.rem(col, ROWS_DEV) // 2
                    right = g_buf[dev, pl.ds(tile * 4, 4)].reshape(BLK, 128)
                    left = l_buf[i, k // 2]
                    if k % 2 == 0:
                        shift = half * BLK
                    else:
                        shift = BLK - half * BLK
                    left = pltpu.roll(left, shift, 1)
                    left = jnp.where((lane >= BLK) == (half == 1), left, zero)
                    prods.append(
                        lax.dot_general(
                            left, right, (((1,), (1,)), ((), ())), preferred_element_type=jnp.float32
                        )
                    )
                for k, prod in zip(range(base, base + 4), prods):
                    seg = seg_ref[i * SLOTS + k]
                    acc[seg] += prod

    for a in range(AGG_DEV):

        @pl.loop(0, window // 2)
        def _(w):
            pair = jnp.concatenate([acc[a * window + 2 * w], acc[a * window + 2 * w + 1]], axis=1)
            out_ref[a, :, pl.ds(pl.multiple_of(w * 128, 128), 128)] = pair


def entries(seg, cols, counts, gathered, left):
    window = 6 * Y * AGG_DEV
    return pl.pallas_call(
        entry_kernel,
        out_shape=jax.ShapeDtypeStruct((AGG_DEV, BLK, window * BLK), jnp.float32),
        in_specs=[pl.BlockSpec(memory_space=pltpu.SMEM)] * 3 + [pl.BlockSpec(memory_space=pl.ANY)] * 2,
        out_specs=pl.BlockSpec(memory_space=pltpu.VMEM),
        scratch_shapes=[
            pltpu.VMEM((6 * Y, PIECE, 16, 128), jnp.bfloat16),
            pltpu.VMEM((ROWS_DEV, LTILES, BLK, 128), jnp.bfloat16),
            pltpu.VMEM((AGG_DEV * window + 1, BLK, BLK), jnp.float32),
            pltpu.SemaphoreType.DMA((6 * Y,)),
            pltpu.SemaphoreType.DMA((ROWS_DEV // 4,)),
        ],
        compiler_params=pltpu.CompilerParams(vmem_limit_bytes=48 << 20),
        name="entries",
    )(seg, cols, counts, gathered, left)


def per_device(matrix_blocks, restrict, columns, counts, aggregate):
    n_rows = lax.axis_size("rows")
    slab_index = lax.axis_index("rows")
    slab_rows = ROWS_DEV * 2 * Y
    window = 6 * Y * AGG_DEV
    tiles = restrict.reshape(TILES, 2, 4, 16, BLK).transpose(0, 2, 3, 1, 4).reshape(TILES * 4, 16, 128)
    agg_tile = jnp.pad(aggregate.astype(jnp.bfloat16)[None, None, :], ((0, 0), (0, 15), (0, 96)))
    piece = jnp.concatenate([tiles, agg_tile], axis=0)
    gathered, left = gather(piece, matrix_blocks, n_rows)
    near_aggs = gathered[:, PIECE - 1, 0, :ROWS_DEV].astype(jnp.int32).reshape(-1)
    inside = ((columns >= slab_rows) | (slab_index > 0)) & (
        (columns < 2 * slab_rows) | (slab_index < n_rows - 1)
    )
    slot_index = jnp.arange(SLOTS, dtype=jnp.int32)
    live = (slot_index[None, :] < counts[:, None]) & inside
    slot_ids = columns // ROWS_DEV * AGG_DEV + near_aggs[columns]
    seg = jnp.where(live, aggregate[:, None] * window + slot_ids, AGG_DEV * window)
    return entries(seg.reshape(-1), columns.reshape(-1), counts, gathered, left)


def solution(mesh):
    return jax.shard_map(
        per_device,
        mesh=mesh,
        in_specs=(
            P(("rows", "cols"), None, None),
            P(("rows", "cols"), None),
            P(("rows", "cols"), None),
            P(("rows", "cols")),
            P(("rows", "cols")),
        ),
        out_specs=P(("rows", "cols"), None, None),
        check_vma=False,
    )
```

time: 339 us -> 110 us (0.32)
  matrix products: 95.9 us -> 0 us
  Pallas kernels: 0 us -> 93.7 us
  waiting for transfers between devices: 74.6 us -> 0 us
  local copies, waits for them, and re-layouts: 80.5 us -> 12.8 us
  blocking collectives: 45.3 us -> 0 us
  starting transfers between devices: 17.5 us -> 0 us
  between operations: 14.2 us -> 0.1 us
  other arithmetic: 7.74 us -> 1.61 us
    dot_general x3 -> x0, matrix products: 95.9 us -> none  [the longest x1 64.2 us: per_device(): jnp.einsum('ikm,ikpq->mpq', one_hot, products, precision=lax.Precision.HI...]
    pallas_call x0 -> x2, Pallas kernels: none -> 93.7 us  [the longest x1 47 us: gather(): pl.pallas_call(functools.partial(gather_kernel, n_rows, with_left), out_s...]
    all_gather x1 -> x0, waiting for transfers between devices: 73.9 us -> none  [per_device(): lax.all_gather(restrict, 'cols', axis=0, tiled=True)]
    unnamed x1 -> x0, blocking collectives: 45.3 us -> none
    reshape x5, local copies, waits for them, and re-layouts: 48.4 us -> 3.19 us  [the longest x3 2.28 us: per_device(): restrict.reshape(TILES, 2, 4, 16, BLK).transpose(0, 2, 3, 1, 4)]
    gather x1 -> x0, local copies, waits for them, and re-layouts: 18.5 us -> none  [per_device(): near_blocks[columns.reshape(-1)].reshape(ROWS_DEV, SLOTS, BLK, BLK)]
    ppermute x4 -> x0, starting transfers between devices: 17.5 us -> none  [the longest x2 11.6 us: padded(): lax.ppermute(lax.slice_in_dim(block, 0, width, axis=dim), axis, backward)]
    concatenate x2 -> x1, other arithmetic: 5.46 us -> 0.02 us  [per_device(): piece = jnp.concatenate([tiles, agg_tile], axis=0)]
  transfers between devices with their start and end apart: 5 -> 0, of which waited for: 1 -> 0; matrix products, arithmetic and copies ran while one was open for 12% -> 0% of each run, Pallas kernels for 0% -> 0%
where the time goes in v1:
time: 110 us; the launch traced here: 108 us
  Pallas kernels  93.7 us (85%)
  local copies, waits for them, and re-layouts  12.8 us (12%)
  other arithmetic  1.61 us (1%)
    pallas_call x1, Pallas kernels, gather(): pl.pallas_call(functools.partial(gather_kernel, n_rows, with_left), out_s...  47 us
    pallas_call x1, Pallas kernels, entries(): pl.pallas_call(entry_kernel, out_shape=jax.ShapeDtypeStruct((AGG_DEV, BLK...  46.6 us
    unnamed x8, local copies, waits for them, and re-layouts  5.68 us
    gather x2, local copies, waits for them, and re-layouts, per_device(): slot_ids = columns // ROWS_DEV * AGG_DEV + near_aggs[columns]  3.76 us
    reshape x3, local copies, waits for them, and re-layouts, per_device(): restrict.reshape(TILES, 2, 4, 16, BLK).transpose(0, 2, 3, 1, 4)  2.28 us

profile of v1, /device:TPU:31, one launch (start us, length us, event | category | flops | bytes accessed | tf_op | source)
XLA Modules:
  0.0 108.2 jit_solution(7521688513397342405)
XLA Ops:
  0.0 0.7 broadcast_multiply_fusion
  0.7 0.8 reshape.22.col_ref
  1.6 0.7 add_select_fusion
  2.3 0.1 reshape.26
  2.4 1.5 %reshape.19 = bf16[16,2,4,16,64]{4,3,2,1,0:T(8,128)(2,1)S(1)} reshape(bf16[32,4096]{1,0:T(8,128)(2,1)} %param.6) | data formatting | bytes 524288 | tf_op jit(solution)/shard_map/reshape | solution.py:353
  3.9 0.5 copy.9
  4.4 0.3 reshape.20
  4.7 47.0 %gather_left.1 = (bf16[24,65,16,128]{3,2,1,0:T(8,128)(2,1)S(1)}, bf16[32,14,64,128]{3,2,1,0:T(8,128)(2,1)S(1)}) custom-call(bf16[65,16,128]{2,1,0:T(8,128)(2,1)S(1)} %fusion.1.x_ref, bf16[32,64,1728]{2,1,0:T(8,128)(2,1)} %a_hbm.1), custom_call_target="tpu_custom_call" | custom-call | tf_op jit(solution)/shard_map/gather_left/pallas_call | solution.py:235
  51.8 0.0 copy-start
  51.8 2.9 %copy-done = bf16[32,14,64,128]{3,2,1,0:T(8,128)(2,1)} copy-done((bf16[32,14,64,128]{3,2,1,0:T(8,128)(2,1)}, bf16[32,14,64,128]{3,2,1,0:T(8,128)(2,1)S(1)}, u32[]{:S(2)}) %copy-start) | copy-done | bytes 7340056
  54.7 0.0 copy-start.1
  54.7 2.7 %copy-done.1 = bf16[24,65,16,128]{3,2,1,0:T(8,128)(2,1)} copy-done((bf16[24,65,16,128]{3,2,1,0:T(8,128)(2,1)}, bf16[24,65,16,128]{3,2,1,0:T(8,128)(2,1)S(1)}, u32[]{:S(2)}) %copy-start.1) | copy-done | bytes 6389784
  57.5 0.1 reshape.23
  57.6 0.0 copy-start.2
  57.6 0.0 copy-start.3
  57.6 3.7 %gather_fusion = s32[864]{0:T(1024)S(1)} fusion(s32[768]{0:T(1024)S(1)} %reshape.23, s32[1024]{0:T(1024)S(1)} %pad_clamp_fusion), kind=kCustom, calls=%fused_computation | custom fusion | bytes 10368 | tf_op jit(solution)/shard_map/gather | solution.py:363
  61.2 0.1 reshape.25
  61.3 0.0 copy-done.2
  61.3 0.0 copy-done.3
  61.3 0.1 fusion.6
  61.4 0.1 reshape.21.seg_ref
  61.5 46.6 %entries.1 = f32[2,64,3072]{2,1,0:T(8,128)} custom-call(s32[864]{0:T(1024)S(1)} %reshape.21.seg_ref, s32[864]{0:T(1024)S(1)} %reshape.22.col_ref, s32[32]{0:T(128)S(1)} %copy-done.2, bf16[24,65,16,128]{3,2,1,0:T(8,128)(2,1)} %copy-done.1, bf16[32,14,64,128]{3,2,1,0:T(8,128)(2,1)} %copy-done), custom_call_target="tpu_custom_call" | custom-call | tf_op jit(solution)/shard_map/entries/pallas_call | solution.py:331
  (3 shorter events, 0.1 us)
Async XLA Ops:
  51.8 3.0 %copy-start = (bf16[32,14,64,128]{3,2,1,0:T(8,128)(2,1)}, bf16[32,14,64,128]{3,2,1,0:T(8,128)(2,1)S(1)}, u32[]{:S(2)}) copy-start(bf16[32,14,64,128]{3,2,1,0:T(8,128)(2,1)S(1)} %get-tuple-element.8.l_hbm) | copy-start | bytes 22020100
  54.7 2.7 %copy-start.1 = (bf16[24,65,16,128]{3,2,1,0:T(8,128)(2,1)}, bf16[24,65,16,128]{3,2,1,0:T(8,128)(2,1)S(1)}, u32[]{:S(2)}) copy-start(bf16[24,65,16,128]{3,2,1,0:T(8,128)(2,1)S(1)} %get-tuple-element.7.g_hbm) | copy-start | bytes 19169284
  57.6 3.8 %copy-start.2 = (s32[32]{0:T(128)S(1)}, s32[32]{0:T(128)}, u32[]{:S(2)}) copy-start(s32[32]{0:T(128)} %count_ref.1) | copy-start | bytes 388
  57.6 3.8 %copy-start.3 = (s32[32,27]{1,0:T(8,128)S(1)}, s32[32,27]{1,0:T(8,128)}, u32[]{:S(2)}) copy-start(s32[32,27]{1,0:T(8,128)} %param.7) | copy-start | bytes 10372
